TPU v7x, 512 devices: a whole 4x8x8 slice. The times are simulated.
512 devices in a mesh: dp: 4 (over x), row: 32 (over y, z_hi, core), col: 4 (over z_lo).
Axes of the slice: x: 4, y: 8, z: 8 (z_hi: 2, z_lo: 4; z = z_hi * 4 + z_lo), core: 2. Of those that a mesh axis runs over, the one named last changes fastest.
Arguments:
- tokens: bfloat16 [2048, 8192], P('dp', ('row', 'col')), may hold values from -6 to 6
- hidden_grad: bfloat16 [2048, 6656], P(('dp', 'row'), 'col'), may hold values from -6 to 6
- gate_weight: bfloat16 [8192, 6656], P('row', 'col'), may hold values from -0.0625 to 0.0625
- up_weight: bfloat16 [8192, 6656], P('row', 'col'), may hold values from -0.0625 to 0.0625
Outputs:
- input_grad: bfloat16 [2048, 8192], P('dp', ('row', 'col'))
- gate_grad: bfloat16 [8192, 6656], P('row', 'col')
- up_grad: bfloat16 [8192, 6656], P('row', 'col')
All inputs are finite; a program needn't handle non-finite values.
Results may differ from a plain program's by a relative error of at most 0.022.
Values may be sent and summed in bfloat16 or wider, within the bound.
A program may use at most 64 MiB of HBM per device.

v0:
```python
import jax
import jax.numpy as jnp
from jax import lax
from jax.sharding import PartitionSpec as P


def contract_rows(left, right):
    return lax.dot_general(
        left, right, (((0,), (0,)), ((), ())), preferred_element_type=jnp.float32
    )


def contract_cols(left, right):
    return lax.dot_general(
        left, right, (((1,), (1,)), ((), ())), preferred_element_type=jnp.float32
    )


def body(tokens, hidden_grad, gate_weight, up_weight):
    panel = lax.all_gather(tokens, "col", axis=1, tiled=True)
    width = gate_weight.shape[1]
    shares = lax.psum_scatter(
        jnp.concatenate(
            [
                jnp.dot(panel, gate_weight, preferred_element_type=jnp.float32),
                jnp.dot(panel, up_weight, preferred_element_type=jnp.float32),
            ],
            axis=1,
        ).astype(jnp.bfloat16),
        "row",
        scatter_dimension=0,
        tiled=True,
    ).astype(jnp.float32)
    gate = shares[:, :width]
    up = shares[:, width:]
    sigma = jax.nn.sigmoid(gate)
    upstream = hidden_grad.astype(jnp.float32)
    gate_act = (upstream * up * sigma * (1.0 + gate * (1.0 - sigma))).astype(jnp.bfloat16)
    up_act = (upstream * gate * sigma).astype(jnp.bfloat16)
    gate_panel, up_panel = (
        lax.all_gather(gate_act, "row", axis=0, tiled=True),
        lax.all_gather(up_act, "row", axis=0, tiled=True),
    )
    input_share = lax.psum_scatter(
        (contract_cols(gate_weight, gate_panel) + contract_cols(up_weight, up_panel)).astype(
            jnp.bfloat16
        ),
        "col",
        scatter_dimension=0,
        tiled=True,
    ).astype(jnp.float32)
    input_grad = input_share.T.astype(jnp.bfloat16)
    gate_local = contract_rows(panel, gate_panel)
    up_local = contract_rows(panel, up_panel)
    gate_sum, up_sum = (
        lax.psum(gate_local.astype(jnp.bfloat16), "dp").astype(jnp.float32),
        lax.psum(up_local.astype(jnp.bfloat16), "dp").astype(jnp.float32),
    )
    return (input_grad, gate_sum.astype(jnp.bfloat16), up_sum.astype(jnp.bfloat16))


def solution(mesh):
    return jax.shard_map(
        body,
        mesh=mesh,
        in_specs=(
            P("dp", ("row", "col")),
            P(("dp", "row"), "col"),
            P("row", "col"),
            P("row", "col"),
        ),
        out_specs=(P("dp", ("row", "col")), P("row", "col"), P("row", "col")),
        check_vma=False,
    )
```

profile of v0, /device:TPU:2, one launch (start us, length us, event | category | flops | bytes accessed | tf_op | source)
XLA Modules:
  0.0 454.6 jit_solution(16732908509172800166)
XLA Ops:
  7.2 0.0 reduce-scatter.5.cloned.1.call-start
  7.2 16.8 %all_gather.9 = bf16[512,256]{0,1:T(8,128)(2,1)S(1)} all-gather(bf16[512,64]{0,1:T(8,128)(2,1)} %param.4), channel_id=1, replica_groups=mesh['dp'=4,'row'=32,'col'=4] {'col'}, dimensions={1}, use_global_device_ids=true | all-gather | bytes 327680 | tf_op jit(solution)/shard_map/all_gather | solution.py:20
  24.0 1.8 convolution_convert_fusion
  25.9 0.7 convolution_convert_fusion.1
  26.5 1.9 pad_maximum_fusion
  28.5 0.0 all-gather.3.cloned.1.call-start
  28.6 149.2 %reduce-scatter.5.cloned.1.call-done = bf16[16,3328]{1,0:T(8,128)(2,1)} async-done(((bf16[512,3328]{1,0:T(8,128)(2,1)}), bf16[16,3328]{1,0:T(8,128)(2,1)}) %reduce-scatter.5.cloned.1.call-update) | async-done | bytes 106512 | tf_op jit(solution)/shard_map/reduce_scatter | solution.py:22
  177.7 0.9 convert_element_type.41
  178.6 0.7 fusion.8
  179.4 0.0 all-gather.5.cloned.1.call-start
  179.4 0.7 all-gather.5.cloned.1.call-update
  180.1 0.0 all-reduce.3.cloned.1.call-start
  180.1 87.8 %all-gather.3.cloned.1.call-done = bf16[512,1664]{1,0:T(8,128)(2,1)} async-done(((bf16[16,1664]{1,0:T(8,128)(2,1)}), bf16[512,1664]{1,0:T(8,128)(2,1)}) %all-gather.3.cloned.1.call-update) | async-done | bytes 1703952 | tf_op jit(solution)/shard_map/all_gather | solution.py:41
  267.9 3.0 fusion
  271.0 86.0 %all-gather.5.cloned.1.call-done = bf16[512,1664]{1,0:T(8,128)(2,1)} async-done(((bf16[16,1664]{1,0:T(8,128)(2,1)}), bf16[512,1664]{1,0:T(8,128)(2,1)}) %all-gather.5.cloned.1.call-update) | async-done | bytes 1703952 | tf_op jit(solution)/shard_map/all_gather | solution.py:42
  357.0 3.0 fusion.1
  360.0 0.0 reduce-scatter.7.cloned.1.call-start
  360.1 2.3 fusion.9
  362.4 1.4 fusion.3
  363.8 1.8 copy.13
  365.6 49.9 %all-reduce.3.cloned.1.call-done = (bf16[256,1664]{0,1:T(8,128)(2,1)}, bf16[256,1664]{0,1:T(8,128)(2,1)}) async-done(((bf16[256,1664]{0,1:T(8,128)(2,1)}, bf16[256,1664]{0,1:T(8,128)(2,1)}), (bf16[256,1664]{0,1:T(8,128)(2,1)}, bf16[256,1664]{0,1:T(8,128)(2,1)})) %all-reduce.3.cloned.1.call-update) | async-done | bytes 1703952 | tf_op jit(solution)/shard_map/psum | solution.py:56
  415.5 2.3 copy.11
  417.8 1.3 copy.12
  419.1 28.9 %reduce-scatter.7.cloned.1.call-done = bf16[64,512]{1,0:T(8,128)(2,1)} async-done(((bf16[256,512]{1,0:T(8,128)(2,1)}), bf16[64,512]{1,0:T(8,128)(2,1)}) %reduce-scatter.7.cloned.1.call-update) | async-done | bytes 65552
  (14 shorter events, 0.1 us)
Async XLA Ops:
  7.2 18.7 %copy-start = (bf16[256,1664]{1,0:T(8,128)(2,1)S(1)}, bf16[256,1664]{1,0:T(8,128)(2,1)}, u32[]{:S(2)}) copy-start(bf16[256,1664]{1,0:T(8,128)(2,1)} %param.6) | copy-start | bytes 2555908
  7.2 170.5 %reduce-scatter.5.cloned.1.call-start = ((), (), s32[]{:S(2)}) async-start(), calls=%async_computation.2 | async-start | bytes 3514368 | tf_op jit(solution)/shard_map/reduce_scatter | solution.py:22
  28.5 150.2 %copy-start.4 = (bf16[16,1664]{1,0:T(8,128)(2,1)S(1)}, bf16[16,1664]{1,0:T(8,128)(2,1)}, u32[]{:S(2)}) copy-start(bf16[16,1664]{1,0:T(8,128)(2,1)} %param.5) | copy-start | bytes 159748
  28.5 239.4 %all-gather.3.cloned.1.call-start = ((), (), s32[]{:S(2)}) async-start(), calls=%async_computation.3 | async-start | bytes 1757184 | tf_op jit(solution)/shard_map/all_gather | solution.py:41
  179.4 177.6 %all-gather.5.cloned.1.call-start = ((), (), s32[]{:S(2)}) async-start(), calls=%async_computation.4 | async-start | bytes 1757184 | tf_op jit(solution)/shard_map/all_gather | solution.py:42
  180.1 235.4 %all-reduce.3.cloned.1.call-start = ((), (), s32[]{:S(2)}) async-start(), calls=%async_computation.6 | async-start | bytes 3407872 | tf_op jit(solution)/shard_map/psum | solution.py:56
  360.0 2.4 copy-start.1
  360.0 2.4 copy-start.2
  360.0 88.0 %reduce-scatter.7.cloned.1.call-start = ((), (), s32[]{:S(2)}) async-start(), calls=%async_computation.5 | async-start | bytes 327680
  415.5 2.3 copy-start.3
Sparse Core Ops, SparseCore 0:
  28.6 149.0 reduce-scatter.4
  181.6 86.3 all-gather.2
  271.8 85.1 all-gather.4
  360.1 55.3 all-reduce.2
  418.7 29.2 reduce-scatter.6
where the time goes:
time: 455 us
  waiting for transfers between devices  403 us (89%)
  blocking collectives  16.8 us (4%)
  between operations  13.9 us (3%)
  matrix products  12.2 us (3%)
  local copies, waits for them, and re-layouts  5.43 us (1%)
    reduce_scatter x1, waiting for transfers between devices, body(): lax.psum_scatter(jnp.concatenate([jnp.dot(panel, gate_weight, preferred_e...  149 us
    all_gather x1, waiting for transfers between devices, body(): lax.all_gather(gate_act, 'row', axis=0, tiled=True)  87.8 us
    all_gather x1, waiting for transfers between devices, body(): lax.all_gather(up_act, 'row', axis=0, tiled=True)  86 us
    psum x1, waiting for transfers between devices, body(): lax.psum(gate_local.astype(jnp.bfloat16), 'dp').astype(jnp.float32)  49.9 us
    unnamed x6, waiting for transfers between devices  29.7 us
    all_gather x1, blocking collectives, body(): panel = lax.all_gather(tokens, 'col', axis=1, tiled=True)  16.8 us
  transfers between devices with their start and end apart: 5, of which 5 were waited for; matrix products, arithmetic and copies ran while one was open for 3% of the time, Pallas kernels for 0%

commit v1 on v0

--- a/solution.py
+++ b/solution.py
@@ -17,6 +17,13 @@
 
 
 def body(tokens, hidden_grad, gate_weight, up_weight):
+
+    def enter_weights(state):
+        state_now = lax.axis_size("row")
+        found_now = jnp.stack(state_now * [state], 0)
+        q_next = lax.all_to_all(found_now, axis_name="row", split_axis=0, concat_axis=0)
+        return jnp.concatenate(q_next, 0)
+
     panel = lax.all_gather(tokens, "col", axis=1, tiled=True)
     width = gate_weight.shape[1]
     shares = lax.psum_scatter(
@@ -38,7 +45,7 @@
     gate_act = (upstream * up * sigma * (1.0 + gate * (1.0 - sigma))).astype(jnp.bfloat16)
     up_act = (upstream * gate * sigma).astype(jnp.bfloat16)
     gate_panel, up_panel = (
-        lax.all_gather(gate_act, "row", axis=0, tiled=True),
+        enter_weights(gate_act),
         lax.all_gather(up_act, "row", axis=0, tiled=True),
     )
     input_share = lax.psum_scatter(

time: 455 us -> 396 us (0.87)
  waiting for transfers between devices: 403 us -> 338 us
  starting transfers between devices: 0.2 us -> 6.17 us
    all_gather x1 -> x0, waiting for transfers between devices: 87.8 us -> none  [body(): lax.all_gather(gate_act, 'row', axis=0, tiled=True)]
    all_to_all x0 -> x1, waiting for transfers between devices: none -> 46.8 us  [enter_weights(): lax.all_to_all(found_now, axis_name='row', split_axis=0, concat_axis=0)]
    all_gather x1, waiting for transfers between devices: 86 us -> 62.1 us  [body(): lax.all_gather(up_act, 'row', axis=0, tiled=True)]
    all_to_all x0 -> x1, starting transfers between devices: none -> 6.01 us  [enter_weights(): lax.all_to_all(found_now, axis_name='row', split_axis=0, concat_axis=0)]
    unnamed x6 -> x5, waiting for transfers between devices: 29.7 us -> 29.7 us
where the time goes in v1:
time: 396 us; the launch traced here: 395 us
  waiting for transfers between devices  338 us (85%)
  blocking collectives  16.8 us (4%)
  between operations  13.9 us (4%)
  matrix products  10.7 us (3%)
  local copies, waits for them, and re-layouts  6.73 us (2%)
  starting transfers between devices  6.17 us (2%)
    reduce_scatter x1, waiting for transfers between devices, body(): lax.psum_scatter(jnp.concatenate([jnp.dot(panel, gate_weight, preferred_e...  149 us
    all_gather x1, waiting for transfers between devices, body(): lax.all_gather(up_act, 'row', axis=0, tiled=True)  62.1 us
    psum x1, waiting for transfers between devices, body(): lax.psum(gate_local.astype(jnp.bfloat16), 'dp').astype(jnp.float32)  49.9 us
    all_to_all x1, waiting for transfers between devices, enter_weights(): lax.all_to_all(found_now, axis_name='row', split_axis=0, concat_axis=0)  46.8 us
    unnamed x5, waiting for transfers between devices  29.7 us
    all_gather x1, blocking collectives, body(): panel = lax.all_gather(tokens, 'col', axis=1, tiled=True)  16.8 us
  transfers between devices with their start and end apart: 5, of which 5 were waited for; matrix products, arithmetic and copies ran while one was open for 3% of the time, Pallas kernels for 0%

profile of v1, /device:TPU:2, one launch (start us, length us, event | category | flops | bytes accessed | tf_op | source)
XLA Modules:
  0.0 395.5 jit_solution(11719735316217172535)
XLA Ops:
  7.2 16.8 %all_gather.6 = bf16[512,256]{0,1:T(8,128)(2,1)S(1)} all-gather(bf16[512,64]{0,1:T(8,128)(2,1)} %param.4), channel_id=1, replica_groups=mesh['dp'=4,'row'=32,'col'=4] {'col'}, dimensions={1}, use_global_device_ids=true | all-gather | bytes 327680 | tf_op jit(solution)/shard_map/all_gather | solution.py:27
  24.0 1.8 convolution_convert_fusion
  25.9 0.7 convolution_convert_fusion.1
  26.5 1.9 pad_maximum_fusion
  28.5 149.2 %reduce-scatter.5.cloned.1.call-done = bf16[16,3328]{1,0:T(8,128)(2,1)} async-done(((bf16[512,3328]{1,0:T(8,128)(2,1)}), bf16[16,3328]{1,0:T(8,128)(2,1)}) %reduce-scatter.5.cloned.1.call-update) | async-done | bytes 106512 | tf_op jit(solution)/shard_map/reduce_scatter | solution.py:29
  177.7 0.9 convert_element_type.41
  178.6 0.7 fusion.8
  179.3 1.3 stack.2
  180.6 6.0 %all-to-all-start = ((bf16[32,16,1664]{2,1,0:T(8,128)(2,1)}), bf16[32,16,1664]{2,1,0:T(8,128)(2,1)S(1)}, u32[]{:S(2)}, u32[]{:S(2)}) async-start(bf16[32,16,1664]{2,1,0:T(8,128)(2,1)} %stack.2), calls=%async_computation.1 | async-start | bytes 3407872 | tf_op jit(solution)/shard_map/all_to_all | solution.py:24
  186.6 0.0 all-gather.2.cloned.1.call-start
  186.7 0.7 all-gather.2.cloned.1.call-update
  187.4 0.0 all-reduce.3.cloned.1.call-start
  187.4 46.8 %all-to-all-done = bf16[32,16,1664]{2,1,0:T(8,128)(2,1)S(1)} async-done(((bf16[32,16,1664]{2,1,0:T(8,128)(2,1)}), bf16[32,16,1664]{2,1,0:T(8,128)(2,1)S(1)}, u32[]{:S(2)}, u32[]{:S(2)}) %all-to-all-start) | async-done | bytes 1703968 | tf_op jit(solution)/shard_map/all_to_all | solution.py:24
  234.2 1.6 fusion
  235.8 62.1 %all-gather.2.cloned.1.call-done = bf16[512,1664]{1,0:T(8,128)(2,1)} async-done(((bf16[16,1664]{1,0:T(8,128)(2,1)}), bf16[512,1664]{1,0:T(8,128)(2,1)}) %all-gather.2.cloned.1.call-update) | async-done | bytes 1703952 | tf_op jit(solution)/shard_map/all_gather | solution.py:49
  297.9 3.0 fusion.1
  300.9 0.0 reduce-scatter.7.cloned.1.call-start
  301.0 2.3 fusion.9
  303.3 1.4 fusion.3
  304.7 1.8 copy.13
  306.5 49.9 %all-reduce.3.cloned.1.call-done = (bf16[256,1664]{0,1:T(8,128)(2,1)}, bf16[256,1664]{0,1:T(8,128)(2,1)}) async-done(((bf16[256,1664]{0,1:T(8,128)(2,1)}, bf16[256,1664]{0,1:T(8,128)(2,1)}), (bf16[256,1664]{0,1:T(8,128)(2,1)}, bf16[256,1664]{0,1:T(8,128)(2,1)})) %all-reduce.3.cloned.1.call-update) | async-done | bytes 1703952 | tf_op jit(solution)/shard_map/psum | solution.py:63
  356.4 2.3 copy.11
  358.7 1.3 copy.12
  360.0 28.9 %reduce-scatter.7.cloned.1.call-done = bf16[64,512]{1,0:T(8,128)(2,1)} async-done(((bf16[256,512]{1,0:T(8,128)(2,1)}), bf16[64,512]{1,0:T(8,128)(2,1)}) %reduce-scatter.7.cloned.1.call-update) | async-done | bytes 65552
  (16 shorter events, 0.1 us)
Async XLA Ops:
  7.2 18.7 %copy-start = (bf16[256,1664]{1,0:T(8,128)(2,1)S(1)}, bf16[256,1664]{1,0:T(8,128)(2,1)}, u32[]{:S(2)}) copy-start(bf16[256,1664]{1,0:T(8,128)(2,1)} %param.6) | copy-start | bytes 2555908
  7.2 170.5 %reduce-scatter.5.cloned.1.call-start = ((), (), s32[]{:S(2)}) async-start(), calls=%async_computation.3 | async-start | bytes 3514368 | tf_op jit(solution)/shard_map/reduce_scatter | solution.py:29
  28.5 150.2 %copy-start.5 = (bf16[16,1664]{1,0:T(8,128)(2,1)S(1)}, bf16[16,1664]{1,0:T(8,128)(2,1)}, u32[]{:S(2)}) copy-start(bf16[16,1664]{1,0:T(8,128)(2,1)} %param.5) | copy-start | bytes 159748
  180.6 53.6 %all-to-all-start = ((bf16[32,16,1664]{2,1,0:T(8,128)(2,1)}), bf16[32,16,1664]{2,1,0:T(8,128)(2,1)S(1)}, u32[]{:S(2)}, u32[]{:S(2)}) async-start(bf16[32,16,1664]{2,1,0:T(8,128)(2,1)} %stack.2), calls=%async_computation.1 | async-start | bytes 3407872 | tf_op jit(solution)/shard_map/all_to_all | solution.py:24
  186.6 111.2 %all-gather.2.cloned.1.call-start = ((), (), s32[]{:S(2)}) async-start(), calls=%async_computation.4 | async-start | bytes 1757184 | tf_op jit(solution)/shard_map/all_gather | solution.py:49
  187.4 169.0 %all-reduce.3.cloned.1.call-start = ((), (), s32[]{:S(2)}) async-start(), calls=%async_computation.6 | async-start | bytes 3407872 | tf_op jit(solution)/shard_map/psum | solution.py:63
  234.2 66.7 %copy-start.2 = (bf16[32,16,1664]{2,1,0:T(8,128)(2,1)}, bf16[32,16,1664]{2,1,0:T(8,128)(2,1)S(1)}, u32[]{:S(2)}) copy-start(bf16[32,16,1664]{2,1,0:T(8,128)(2,1)S(1)} %all-to-all-done) | copy-start | bytes 5111812
  300.9 2.4 copy-start.1
  300.9 2.4 copy-start.3
  300.9 88.0 %reduce-scatter.7.cloned.1.call-start = ((), (), s32[]{:S(2)}) async-start(), calls=%async_computation.5 | async-start | bytes 327680
  356.4 2.3 copy-start.4
Sparse Core Ops, SparseCore 0:
  28.6 149.0 reduce-scatter.4
  191.3 106.5 all-gather.1
  301.0 55.3 all-reduce.2
  359.6 29.2 reduce-scatter.6

commit v2 on v0

--- a/solution.py
+++ b/solution.py
@@ -1,7 +1,15 @@
+import functools
 import jax
 import jax.numpy as jnp
 from jax import lax
 from jax.sharding import PartitionSpec as P
+
+
+def resolve_node_up(local_block, axis_key):
+    return jnp.sum(lax.all_gather(local_block, axis_key), 0)
+
+
+tell_the_grid = functools.partial(resolve_node_up, axis_key="dp")
 
 
 def contract_rows(left, right):
@@ -53,7 +61,7 @@
     gate_local = contract_rows(panel, gate_panel)
     up_local = contract_rows(panel, up_panel)
     gate_sum, up_sum = (
-        lax.psum(gate_local.astype(jnp.bfloat16), "dp").astype(jnp.float32),
+        tell_the_grid(gate_local.astype(jnp.bfloat16)).astype(jnp.float32),
         lax.psum(up_local.astype(jnp.bfloat16), "dp").astype(jnp.float32),
     )
     return (input_grad, gate_sum.astype(jnp.bfloat16), up_sum.astype(jnp.bfloat16))

time: 455 us -> 502 us (1.10)
  waiting for transfers between devices: 403 us -> 434 us
  other arithmetic: 3.55 us -> 12.9 us
  local copies, waits for them, and re-layouts: 5.43 us -> 11.9 us
    all_gather x0 -> x1, waiting for transfers between devices: none -> 51.5 us  [resolve_node_up(): return jnp.sum(lax.all_gather(local_block, axis_key), 0)]
    unnamed x6 -> x7, waiting for transfers between devices: 29.7 us -> 15.8 us
    reduce_sum x0 -> x1, other arithmetic: none -> 9.35 us  [resolve_node_up(): return jnp.sum(lax.all_gather(local_block, axis_key), 0)]
    all_gather x0 -> x1, local copies, waits for them, and re-layouts: none -> 7.43 us  [resolve_node_up(): return jnp.sum(lax.all_gather(local_block, axis_key), 0)]
    psum x1, waiting for transfers between devices: 49.9 us -> 44 us  [body(): lax.psum(up_local.astype(jnp.bfloat16), 'dp').astype(jnp.float32)]
  transfers between devices with their start and end apart: 5 -> 6, of which waited for: 5 -> 6; matrix products, arithmetic and copies ran while one was open for 3% -> 6% of each run, Pallas kernels for 0% -> 0%
where the time goes in v2:
time: 502 us
  waiting for transfers between devices  434 us (86%)
  blocking collectives  16.8 us (3%)
  between operations  14.2 us (3%)
  other arithmetic  12.9 us (3%)
  local copies, waits for them, and re-layouts  11.9 us (2%)
  matrix products  11.5 us (2%)
    reduce_scatter x1, waiting for transfers between devices, body(): lax.psum_scatter(jnp.concatenate([jnp.dot(panel, gate_weight, preferred_e...  149 us
    all_gather x1, waiting for transfers between devices, body(): lax.all_gather(up_act, 'row', axis=0, tiled=True)  87.8 us
    all_gather x1, waiting for transfers between devices, body(): lax.all_gather(gate_act, 'row', axis=0, tiled=True)  85.9 us
    all_gather x1, waiting for transfers between devices, resolve_node_up(): return jnp.sum(lax.all_gather(local_block, axis_key), 0)  51.5 us
    psum x1, waiting for transfers between devices, body(): lax.psum(up_local.astype(jnp.bfloat16), 'dp').astype(jnp.float32)  44 us
    all_gather x1, blocking collectives, body(): panel = lax.all_gather(tokens, 'col', axis=1, tiled=True)  16.8 us
    unnamed x7, waiting for transfers between devices  15.8 us
  transfers between devices with their start and end apart: 6, of which 6 were waited for; matrix products, arithmetic and copies ran while one was open for 6% of the time, Pallas kernels for 0%

profile of v2, /device:TPU:2, one launch (start us, length us, event | category | flops | bytes accessed | tf_op | source)
XLA Modules:
  0.0 501.7 jit_solution(2145514143370672330)
XLA Ops:
  7.2 16.8 %all_gather.15 = bf16[512,256]{0,1:T(8,128)(2,1)S(1)} all-gather(bf16[512,64]{0,1:T(8,128)(2,1)} %param.4), channel_id=1, replica_groups=mesh['dp'=4,'row'=32,'col'=4] {'col'}, dimensions={1}, use_global_device_ids=true | all-gather | bytes 327680 | tf_op jit(solution)/shard_map/all_gather | solution.py:28
  24.0 1.8 convolution_convert_fusion
  25.9 0.7 convolution_convert_fusion.1
  26.5 1.9 pad_maximum_fusion
  28.5 0.0 all-gather.7.cloned.1.call-start
  28.6 149.2 %reduce-scatter.5.cloned.1.call-done = bf16[16,3328]{1,0:T(8,128)(2,1)} async-done(((bf16[512,3328]{1,0:T(8,128)(2,1)}), bf16[16,3328]{1,0:T(8,128)(2,1)}) %reduce-scatter.5.cloned.1.call-update) | async-done | bytes 106512 | tf_op jit(solution)/shard_map/reduce_scatter | solution.py:30
  177.7 0.9 convert_element_type.43
  178.6 0.7 fusion.8
  179.4 0.7 all-gather.5.cloned.1.call-update
  180.2 87.8 %all-gather.7.cloned.1.call-done = bf16[512,1664]{1,0:T(8,128)(2,1)} async-done(((bf16[16,1664]{1,0:T(8,128)(2,1)}), bf16[512,1664]{1,0:T(8,128)(2,1)}) %all-gather.7.cloned.1.call-update) | async-done | bytes 1703952 | tf_op jit(solution)/shard_map/all_gather | solution.py:50
  268.0 3.0 fusion.1
  271.0 0.0 all-gather.9.cloned.1.call-start
  271.0 85.9 %all-gather.5.cloned.1.call-done = bf16[512,1664]{1,0:T(8,128)(2,1)} async-done(((bf16[16,1664]{1,0:T(8,128)(2,1)}), bf16[512,1664]{1,0:T(8,128)(2,1)}) %all-gather.5.cloned.1.call-update) | async-done | bytes 1703952 | tf_op jit(solution)/shard_map/all_gather | solution.py:49
  357.0 3.0 fusion
  360.1 2.3 fusion.9
  362.4 0.7 fusion.3
  363.1 0.9 copy.12
  364.0 44.0 %all-reduce.2.cloned.1.call-done = bf16[256,1664]{0,1:T(8,128)(2,1)} async-done(((bf16[256,1664]{0,1:T(8,128)(2,1)}), bf16[256,1664]{0,1:T(8,128)(2,1)}) %all-reduce.2.cloned.1.call-update) | async-done | bytes 851984 | tf_op jit(solution)/shard_map/psum | solution.py:65
  408.0 2.2 copy.11
  410.2 51.5 %all-gather.9.cloned.1.call-done = bf16[1024,1664]{0,1:T(8,128)(2,1)} async-done(((bf16[256,1664]{0,1:T(8,128)(2,1)}), bf16[1024,1664]{0,1:T(8,128)(2,1)}) %all-gather.9.cloned.1.call-update) | async-done | bytes 3407888 | tf_op jit(solution)/shard_map/all_gather | solution.py:9
  461.7 7.4 %reshape.6 = bf16[4,256,1664]{1,0,2:T(4,128)(2,1)} reshape(bf16[1024,1664]{0,1:T(8,128)(2,1)} %all-gather.9.cloned.1.call-done) | data formatting | bytes 6815744 | tf_op jit(solution)/shard_map/all_gather | solution.py:9
  469.1 9.3 %reduce_sum.12 = bf16[256,1664]{0,1:T(8,128)(2,1)S(1)} reduce(bf16[4,256,1664]{1,0,2:T(4,128)(2,1)} %reshape.6, bf16[]{:T(256)} %constant.4.clone.1), dimensions={0}, to_apply=%region_2.0 | reduce | flops 1277952 | bytes 4259842 | tf_op jit(solution)/shard_map/reduce_sum | solution.py:9
  478.5 1.4 copy.10
  479.8 15.0 %reduce-scatter.7.cloned.1.call-done = bf16[64,512]{1,0:T(8,128)(2,1)} async-done(((bf16[256,512]{1,0:T(8,128)(2,1)}), bf16[64,512]{1,0:T(8,128)(2,1)}) %reduce-scatter.7.cloned.1.call-update) | async-done | bytes 65552
  (17 shorter events, 0.3 us)
Async XLA Ops:
  7.2 18.7 %copy-start = (bf16[256,1664]{1,0:T(8,128)(2,1)S(1)}, bf16[256,1664]{1,0:T(8,128)(2,1)}, u32[]{:S(2)}) copy-start(bf16[256,1664]{1,0:T(8,128)(2,1)} %param.6) | copy-start | bytes 2555908
  7.2 170.5 %reduce-scatter.5.cloned.1.call-start = ((), (), s32[]{:S(2)}) async-start(), calls=%async_computation.2 | async-start | bytes 3514368 | tf_op jit(solution)/shard_map/reduce_scatter | solution.py:30
  28.5 150.2 %copy-start.3 = (bf16[16,1664]{1,0:T(8,128)(2,1)S(1)}, bf16[16,1664]{1,0:T(8,128)(2,1)}, u32[]{:S(2)}) copy-start(bf16[16,1664]{1,0:T(8,128)(2,1)} %param.5) | copy-start | bytes 159748
  28.5 239.4 %all-gather.7.cloned.1.call-start = ((), (), s32[]{:S(2)}) async-start(), calls=%async_computation.4 | async-start | bytes 1757184 | tf_op jit(solution)/shard_map/all_gather | solution.py:50
  179.4 177.6 %all-gather.5.cloned.1.call-start = ((), (), s32[]{:S(2)}) async-start(), calls=%async_computation.3 | async-start | bytes 1757184 | tf_op jit(solution)/shard_map/all_gather | solution.py:49
  180.1 227.9 %all-reduce.2.cloned.1.call-start = ((), (), s32[]{:S(2)}) async-start(), calls=%async_computation.5 | async-start | bytes 1703936 | tf_op jit(solution)/shard_map/psum | solution.py:65
  271.0 190.7 %all-gather.9.cloned.1.call-start = ((), (), s32[]{:S(2)}) async-start(), calls=%async_computation.6 | async-start | bytes 4259840 | tf_op jit(solution)/shard_map/all_gather | solution.py:9
  360.0 2.4 copy-start.1
  360.0 134.8 %reduce-scatter.7.cloned.1.call-start = ((), (), s32[]{:S(2)}) async-start(), calls=%async_computation.7 | async-start | bytes 327680
  360.1 2.3 copy-start.2
Sparse Core Ops, SparseCore 0:
  28.6 149.0 reduce-scatter.4
  181.6 86.3 all-gather.6
  271.8 85.1 all-gather.4
  359.8 48.1 all-reduce.1
  410.5 51.1 all-gather.8
  464.9 29.8 reduce-scatter.6
